TPU v7x, 512 devices: a whole 4x4x16 slice. The times are simulated.
512 devices in a mesh: seq: 32 (over z, core), heads: 4 (over x), dp: 4 (over y).
Axes of the slice: x: 4, y: 4, z: 16, core: 2. Of those that a mesh axis runs over, the one named last changes fastest.
Arguments:
- tokens: bfloat16 [4, 4096, 3072], P('dp', 'seq'), may hold values from -6 to 6
- proj_weights: bfloat16 [3, 3072, 4096], P(None, 'seq', ('heads', 'dp')), may hold values from -0.109375 to 0.109375
- norm_gain: float32 [4096], P(('heads', 'dp')), may hold values from 0.5 to 1.5
Outputs:
- attended: bfloat16 [4, 4096, 4096], P('dp', 'seq', 'heads')
All inputs are finite; a program needn't handle non-finite values.
Results may differ from a plain program's by a relative error of at most 0.0063.
Values may be sent and summed in bfloat16 or wider, within the bound.
No kernel may reach another device: no remote copies, remote signals or barrier semaphores. Data moves between devices by JAX's collectives and lax.ppermute only.
A program may use at most 64 MiB of HBM per device.

v0:
```python
import jax
import jax.numpy as jnp
from jax import lax
from jax.sharding import PartitionSpec as P

DH = 128


def prefix_2(part, axis, combine, identity):
    place = lax.axis_index(axis)
    gathered = lax.all_gather(part, axis)
    state = jnp.zeros_like(part) + jnp.asarray(identity, part.dtype)

    def one(step, state):
        return combine(state, lax.dynamic_index_in_dim(gathered, step, 0, False))

    return lax.fori_loop(0, place, one, state)


def add_pair(earlier, later):
    return earlier + later


def project_rows(flat_rows):

    def accumulate(total, piece, start):
        return jnp.einsum("nd,jdc->jnc", flat_rows, piece, preferred_element_type=jnp.float32)

    return accumulate


def to_heads(matrix, seq_count, length):
    return matrix.reshape(seq_count, length, -1, DH)


def activate(matrix, seq_count, length):
    return to_heads(jax.nn.silu(matrix).astype(jnp.bfloat16), seq_count, length)


def block_prefix(keys_b, values_b):
    state = jnp.einsum("sthd,sthe->shde", keys_b, values_b, preferred_element_type=jnp.float32)
    return prefix_2(state, "seq", add_pair, jnp.zeros_like(state))


def attend(queries, keys_b, values_b, prefix, norm_gain):
    seq_count, length, head_count, head_size = queries.shape
    scores = jnp.einsum("sthd,suhd->shtu", queries, keys_b, preferred_element_type=jnp.float32)
    causal = lax.broadcasted_iota(jnp.int32, (length, length), 0) >= lax.broadcasted_iota(
        jnp.int32, (length, length), 1
    )
    scores_b = jnp.where(causal, scores, 0.0).astype(jnp.bfloat16)
    local = jnp.einsum("shtu,suhd->sthd", scores_b, values_b, preferred_element_type=jnp.float32)
    carried = jnp.einsum(
        "sthd,shde->sthe", queries, prefix.astype(jnp.bfloat16), preferred_element_type=jnp.float32
    )
    attn = local + carried
    scale = lax.rsqrt(jnp.mean(attn * attn, axis=-1, keepdims=True) + 1e-06)
    normed = attn * scale * norm_gain.reshape(head_count, head_size)
    return normed.astype(jnp.bfloat16).reshape(seq_count, length, head_count * head_size)


def body(tokens, proj_weights, norm_gain):
    everyone = lax.all_gather(tokens, "dp", axis=0, tiled=True)
    seq_count, length, width = everyone.shape
    total_rows = seq_count * length
    per_device = proj_weights.shape[2]
    accumulate = project_rows(everyone.reshape(total_rows, width))
    start_sum = jnp.zeros((3, total_rows, per_device), jnp.float32)
    projected = accumulate(
        start_sum, lax.all_gather(proj_weights, "seq", axis=1, tiled=True), jnp.int32(0)
    )
    queries = activate(projected[0], seq_count, length)
    keys_b = activate(projected[1], seq_count, length)
    values_b = to_heads(projected[2].astype(jnp.bfloat16), seq_count, length)
    prefix = block_prefix(keys_b, values_b)
    normed = attend(queries, keys_b, values_b, prefix, norm_gain)
    return lax.all_to_all(normed, "dp", split_axis=0, concat_axis=2, tiled=True)


def solution(mesh):
    in_specs = (P("dp", "seq", None), P(None, "seq", ("heads", "dp")), P(("heads", "dp")))
    out_specs = P("dp", "seq", "heads")
    return jax.shard_map(body, mesh=mesh, in_specs=in_specs, out_specs=out_specs, check_vma=False)
```

profile of v0, /device:TPU:481, one launch (start us, length us, event | category | flops | bytes accessed | tf_op | source)
XLA Modules:
  0.0 297.7 jit_solution(694654217346947341)
XLA Ops:
  6.5 0.7 all-gather.7.cloned.1.call-update
  7.3 0.7 all-gather.5.cloned.1.call-update
  8.1 47.7 %all-gather.7.cloned.1.call-done = bf16[4,128,3072]{2,1,0:T(8,128)(2,1)} async-done(((bf16[1,128,3072]{2,1,0:T(8,128)(2,1)}), bf16[4,128,3072]{2,1,0:T(8,128)(2,1)}) %all-gather.7.cloned.1.call-update) | async-done | bytes 3145744 | tf_op jit(solution)/shard_map/all_gather | solution.py:63
  55.8 76.4 %all-gather.5.cloned.1.call-done = bf16[3,3072,256]{2,1,0:T(8,128)(2,1)} async-done(((bf16[3,96,256]{2,1,0:T(8,128)(2,1)}), bf16[3,3072,256]{2,1,0:T(8,128)(2,1)}) %all-gather.5.cloned.1.call-update) | async-done | bytes 4718608 | tf_op jit(solution)/shard_map/all_gather | solution.py:70
  132.1 5.5 %convolution_bitcast_fusion = f32[3,512,256]{1,2,0:T(8,128)S(1)} fusion(bf16[3,3072,256]{2,1,0:T(8,128)(2,1)} %all-gather.5.cloned.1.call-done, bf16[512,3072,1]{1,0,2:T(8,128)(2,1)} %bitcast.33), kind=kOutput, calls=%fused_computation.1 | convolution fusion | flops 2415919104 | bytes 9437184 | tf_op jit(solution)/shard_map/nd,jdc->jnc/dot_general | solution.py:27
  137.7 0.2 squeeze.12
  137.9 0.2 copy.16
  138.2 0.2 copy.19
  138.4 1.1 fusion.7
  139.6 0.2 squeeze.11
  139.8 0.2 copy.14
  140.0 0.6 fusion.2
  140.6 101.5 %all-gather.9.cloned.1.call-done = f32[128,2,128,128]{3,2,1,0:T(8,128)} async-done(((f32[4,2,128,128]{3,2,1,0:T(8,128)}), f32[128,2,128,128]{3,2,1,0:T(8,128)}) %all-gather.9.cloned.1.call-update) | async-done | bytes 16777232 | tf_op jit(solution)/shard_map/all_gather | solution.py:11
  242.2 37.0 %while.10 = (s32[]{:T(128)}, f32[4,2,128,128]{3,2,1,0:T(8,128)S(1)}, s32[]{:T(128)}, f32[32,4,2,128,128]{4,3,2,1,0:T(8,128)}, s32[]{:T(128)}, /*index=5*/s32[]{:T(128)}, s32[]{:T(128)}) while((s32[]{:T(128)}, f32[4,2,128,128]{3,2,1,0:T(8,128)S(1)}, s32[]{:T(128)}, f32[32,4,2,128,128]{4,3,2,1,0:T(8,128)}, s32[]{:T(128)}, /*index=5*/s32[]{:T(128)}, ...), condition=%wide.region_1.2_spmd, body=%wide.region_0.1_spmd.sunk | while | flops 131077 | bytes 1572987 | solution.py:17
  242.2 1.2 bitcast_add_fusion.2
  243.4 1.2 bitcast_add_fusion.2
  244.6 1.2 bitcast_add_fusion.2
  245.8 1.2 bitcast_add_fusion.2
  247.0 1.2 bitcast_add_fusion.2
  248.2 1.2 bitcast_add_fusion.2
  249.3 1.2 bitcast_add_fusion.2
  250.5 1.2 bitcast_add_fusion.2
  251.7 1.2 bitcast_add_fusion.2
  252.9 1.2 bitcast_add_fusion.2
  254.1 1.2 bitcast_add_fusion.2
  255.3 1.2 bitcast_add_fusion.2
  256.5 1.2 bitcast_add_fusion.2
  257.7 1.2 bitcast_add_fusion.2
  258.9 1.2 bitcast_add_fusion.2
  260.1 1.2 bitcast_add_fusion.2
  261.3 1.2 bitcast_add_fusion.2
  262.5 1.2 bitcast_add_fusion.2
  263.7 1.2 bitcast_add_fusion.2
  264.9 1.2 bitcast_add_fusion.2
  266.0 1.2 bitcast_add_fusion.2
  267.2 1.2 bitcast_add_fusion.2
  268.4 1.2 bitcast_add_fusion.2
  269.6 1.2 bitcast_add_fusion.2
  270.8 1.2 bitcast_add_fusion.2
  272.0 1.2 bitcast_add_fusion.2
  273.2 1.2 bitcast_add_fusion.2
  274.4 1.2 bitcast_add_fusion.2
  275.6 1.2 bitcast_add_fusion.2
  276.8 1.2 bitcast_add_fusion.2
  278.0 1.2 bitcast_add_fusion.2
  279.2 0.4 multiply_reduce_fusion
  279.7 10.6 %all_to_all.18 = bf16[4,128,256]{1,2,0:T(8,128)(2,1)S(1)} all-to-all(bf16[4,128,256]{1,2,0:T(8,128)(2,1)S(1)} %bitcast.29), channel_id=1, replica_groups=mesh['seq'=32,'heads'=4,'dp'=4] {'dp'}, dimensions={0} | all-to-all | bytes 524288 | tf_op jit(solution)/shard_map/all_to_all | solution.py:77
  290.3 0.8 copy.24
  (13 shorter events, 0.4 us)
Async XLA Ops:
  6.5 49.2 %all-gather.7.cloned.1.call-start = ((), (), s32[]{:S(2)}) async-start(), calls=%async_computation.2 | async-start | bytes 3932160 | tf_op jit(solution)/shard_map/all_gather | solution.py:63
  7.3 124.9 %all-gather.5.cloned.1.call-start = ((), (), s32[]{:S(2)}) async-start(), calls=%async_computation.1 | async-start | bytes 4866048 | tf_op jit(solution)/shard_map/all_gather | solution.py:70
  8.0 234.1 %all-gather.9.cloned.1.call-start = ((), (), s32[]{:S(2)}) async-start(), calls=%async_computation.3 | async-start | bytes 17301504 | tf_op jit(solution)/shard_map/all_gather | solution.py:11
  242.1 37.4 %copy-start = (f32[256]{0:T(256)S(1)}, f32[256]{0:T(256)}, u32[]{:S(2)}) copy-start(f32[256]{0:T(256)} %param.7) | copy-start | bytes 3076
Sparse Core Ops, SparseCore 0:
  9.5 46.2 all-gather.6
  57.9 74.1 all-gather.4
  139.7 102.3 all-gather.8
where the time goes:
time: 299 us; the launch traced here: 298 us
  waiting for transfers between devices  227 us (76%)
  other arithmetic  36.4 us (12%)
  between operations  13.2 us (4%)
  blocking collectives  10.6 us (4%)
  matrix products  7.57 us (3%)
    all_gather x1, waiting for transfers between devices, prefix_2(): gathered = lax.all_gather(part, axis)  101 us
    all_gather x1, waiting for transfers between devices, body(): lax.all_gather(proj_weights, 'seq', axis=1, tiled=True)  76.4 us
    all_gather x1, waiting for transfers between devices, body(): everyone = lax.all_gather(tokens, 'dp', axis=0, tiled=True)  47.7 us
    add x31, other arithmetic, add_pair(): return earlier + later  36.3 us
    all_to_all x1, blocking collectives, body(): return lax.all_to_all(normed, 'dp', split_axis=0, concat_axis=2, tiled=True)  10.6 us
  transfers between devices with their start and end apart: 3, of which 3 were waited for; matrix products, arithmetic and copies ran while one was open for 0% of the time, Pallas kernels for 0%

commit v1 on v0

--- a/solution.py
+++ b/solution.py
@@ -60,7 +60,23 @@
 
 
 def body(tokens, proj_weights, norm_gain):
-    everyone = lax.all_gather(tokens, "dp", axis=0, tiled=True)
+    size, index, rows = (lax.axis_size("dp"), lax.axis_index("dp"), tokens.shape[0])
+    right = [(i, (i + 1) % size) for i in range(size)]
+    left = [(i, (i - 1) % size) for i in range(size)]
+    everyone = jnp.zeros((*tokens.shape[:0], size * rows, *tokens.shape[0 + 1 :]), tokens.dtype)
+    everyone = lax.dynamic_update_slice_in_dim(everyone, tokens, index * rows, axis=0)
+    from_left = from_right = tokens
+    half = size // 2
+    for k in range(1, half + 1):
+        from_left = lax.ppermute(from_left, "dp", right)
+        everyone = lax.dynamic_update_slice_in_dim(
+            everyone, from_left, (index - k) % size * rows, axis=0
+        )
+        if k < size - half:
+            from_right = lax.ppermute(from_right, "dp", left)
+            everyone = lax.dynamic_update_slice_in_dim(
+                everyone, from_right, (index + k) % size * rows, axis=0
+            )
     seq_count, length, width = everyone.shape
     total_rows = seq_count * length
     per_device = proj_weights.shape[2]

time: 299 us -> 249 us (0.83)
  waiting for transfers between devices: 227 us -> 165 us
  starting transfers between devices: 0.08 us -> 8.52 us
  local copies, waits for them, and re-layouts: 2.07 us -> 5.68 us
    all_gather x1 -> x0, waiting for transfers between devices: 47.7 us -> none  [body(): everyone = lax.all_gather(tokens, 'dp', axis=0, tiled=True)]
    all_gather x1, waiting for transfers between devices: 76.4 us -> 31 us  [body(): lax.all_gather(proj_weights, 'seq', axis=1, tiled=True)]
    ppermute x0 -> x3, waiting for transfers between devices: none -> 31.5 us  [the longest x2 31.5 us: body(): from_left = lax.ppermute(from_left, 'dp', right)]
    ppermute x0 -> x3, starting transfers between devices: none -> 8.48 us  [the longest x2 5.12 us: body(): from_left = lax.ppermute(from_left, 'dp', right)]
    dynamic_update_slice x0 -> x4, local copies, waits for them, and re-layouts: none -> 3.71 us  [the longest x2 2.42 us: body(): lax.dynamic_update_slice_in_dim(everyone, from_left, (index - k) % size *...]
  transfers between devices with their start and end apart: 3 -> 5, of which waited for: 3 -> 4; matrix products, arithmetic and copies ran while one was open for 0% -> 2% of each run, Pallas kernels for 0% -> 0%
where the time goes in v1:
time: 249 us; the launch traced here: 247 us
  waiting for transfers between devices  165 us (66%)
  other arithmetic  36.4 us (15%)
  between operations  13.6 us (5%)
  blocking collectives  10.6 us (4%)
  starting transfers between devices  8.52 us (3%)
  matrix products  7 us (3%)
  local copies, waits for them, and re-layouts  5.68 us (2%)
    all_gather x1, waiting for transfers between devices, prefix_2(): gathered = lax.all_gather(part, axis)  102 us
    add x31, other arithmetic, add_pair(): return earlier + later  36.3 us
    ppermute x2, waiting for transfers between devices, body(): from_left = lax.ppermute(from_left, 'dp', right)  31.5 us
    all_gather x1, waiting for transfers between devices, body(): lax.all_gather(proj_weights, 'seq', axis=1, tiled=True)  31 us
    all_to_all x1, blocking collectives, body(): return lax.all_to_all(normed, 'dp', split_axis=0, concat_axis=2, tiled=True)  10.6 us
    ppermute x2, starting transfers between devices, body(): from_left = lax.ppermute(from_left, 'dp', right)  5.12 us
  transfers between devices with their start and end apart: 5, of which 4 were waited for; matrix products, arithmetic and copies ran while one was open for 2% of the time, Pallas kernels for 0%

profile of v1, /device:TPU:481, one launch (start us, length us, event | category | flops | bytes accessed | tf_op | source)
XLA Modules:
  0.0 247.5 jit_solution(10622822817110883523)
XLA Ops:
  6.5 0.7 all-gather.4.cloned.1.call-update
  7.3 3.2 %collective-permute-start = (bf16[1,128,3072]{2,1,0:T(8,128)(2,1)}, bf16[1,128,3072]{2,1,0:T(8,128)(2,1)}, u32[]{:S(2)}, u32[]{:S(2)}) collective-permute-start(bf16[1,128,3072]{2,1,0:T(8,128)(2,1)} %param.5), channel_id=1, source_target_pairs={{0,1},{1,2},{2,3},{3,0},{4,5},{5,6},{6,7},{7,4},{8,9},{9,10},{10,1... | collective-permute-start | bytes 2359304 | tf_op jit(solution)/shard_map/ppermute | solution.py:71
  10.5 3.4 %collective-permute-start.1 = (bf16[1,128,3072]{2,1,0:T(8,128)(2,1)}, bf16[1,128,3072]{2,1,0:T(8,128)(2,1)}, u32[]{:S(2)}, u32[]{:S(2)}) collective-permute-start(bf16[1,128,3072]{2,1,0:T(8,128)(2,1)} %param.5), channel_id=1, source_target_pairs={{0,3},{1,0},{2,1},{3,2},{4,7},{5,4},{6,5},{7,6},{8,11},{9,8},{10,9... | collective-permute-start | bytes 2359304 | tf_op jit(solution)/shard_map/ppermute | solution.py:76
  13.9 15.4 %collective-permute-done = bf16[1,128,3072]{2,1,0:T(8,128)(2,1)} collective-permute-done((bf16[1,128,3072]{2,1,0:T(8,128)(2,1)}, bf16[1,128,3072]{2,1,0:T(8,128)(2,1)}, u32[]{:S(2)}, u32[]{:S(2)}) %collective-permute-start) | collective-permute-done | bytes 786464 | tf_op jit(solution)/shard_map/ppermute | solution.py:71
  29.3 1.9 collective-permute-start.2
  31.7 1.2 constant_dynamic-update-slice_fusion.2
  33.0 1.2 constant_dynamic-update-slice_fusion.1
  34.2 16.1 %collective-permute-done.2 = bf16[1,128,3072]{2,1,0:T(8,128)(2,1)} collective-permute-done((bf16[1,128,3072]{2,1,0:T(8,128)(2,1)}, bf16[1,128,3072]{2,1,0:T(8,128)(2,1)}, u32[]{:S(2)}, u32[]{:S(2)}) %collective-permute-start.2) | collective-permute-done | bytes 786464 | tf_op jit(solution)/shard_map/ppermute | solution.py:71
  50.3 1.2 constant_dynamic-update-slice_fusion
  51.5 31.0 %all-gather.4.cloned.1.call-done = bf16[3,3072,256]{2,1,0:T(8,128)(2,1)} async-done(((bf16[3,96,256]{2,1,0:T(8,128)(2,1)}), bf16[3,3072,256]{2,1,0:T(8,128)(2,1)}) %all-gather.4.cloned.1.call-update) | async-done | bytes 4718608 | tf_op jit(solution)/shard_map/all_gather | solution.py:86
  82.5 4.9 %convolution_bitcast_fusion = f32[3,512,256]{2,1,0:T(8,128)S(1)} fusion(bf16[512,3072,1]{1,0,2:T(8,128)(2,1)S(1)} %bitcast.21, bf16[3,3072,256]{2,1,0:T(8,128)(2,1)} %all-gather.4.cloned.1.call-done), kind=kOutput, calls=%fused_computation.1 | convolution fusion | flops 2415919104 | bytes 9437184 | tf_op jit(solution)/shard_map/nd,jdc->jnc/dot_general | solution.py:27
  87.9 1.1 fusion.7
  89.3 0.6 fusion.2
  89.9 101.7 %all-gather.6.cloned.1.call-done = f32[128,2,128,128]{3,2,1,0:T(8,128)} async-done(((f32[4,2,128,128]{3,2,1,0:T(8,128)}), f32[128,2,128,128]{3,2,1,0:T(8,128)}) %all-gather.6.cloned.1.call-update) | async-done | bytes 16777232 | tf_op jit(solution)/shard_map/all_gather | solution.py:11
  191.6 37.0 %while.10 = (s32[]{:T(128)}, f32[4,2,128,128]{3,2,1,0:T(8,128)S(1)}, s32[]{:T(128)}, f32[32,4,2,128,128]{4,3,2,1,0:T(8,128)}, s32[]{:T(128)}, /*index=5*/s32[]{:T(128)}, s32[]{:T(128)}) while((s32[]{:T(128)}, f32[4,2,128,128]{3,2,1,0:T(8,128)S(1)}, s32[]{:T(128)}, f32[32,4,2,128,128]{4,3,2,1,0:T(8,128)}, s32[]{:T(128)}, /*index=5*/s32[]{:T(128)}, ...), condition=%wide.region_1.2_spmd, body=%wide.region_0.1_spmd.sunk | while | flops 131077 | bytes 1572987 | solution.py:17
  191.7 1.2 bitcast_add_fusion.2
  192.9 1.2 bitcast_add_fusion.2
  194.1 1.2 bitcast_add_fusion.2
  195.2 1.2 bitcast_add_fusion.2
  196.4 1.2 bitcast_add_fusion.2
  197.6 1.2 bitcast_add_fusion.2
  198.8 1.2 bitcast_add_fusion.2
  200.0 1.2 bitcast_add_fusion.2
  201.2 1.2 bitcast_add_fusion.2
  202.4 1.2 bitcast_add_fusion.2
  203.6 1.2 bitcast_add_fusion.2
  204.8 1.2 bitcast_add_fusion.2
  206.0 1.2 bitcast_add_fusion.2
  207.2 1.2 bitcast_add_fusion.2
  208.4 1.2 bitcast_add_fusion.2
  209.6 1.2 bitcast_add_fusion.2
  210.8 1.2 bitcast_add_fusion.2
  212.0 1.2 bitcast_add_fusion.2
  213.1 1.2 bitcast_add_fusion.2
  214.3 1.2 bitcast_add_fusion.2
  215.5 1.2 bitcast_add_fusion.2
  216.7 1.2 bitcast_add_fusion.2
  217.9 1.2 bitcast_add_fusion.2
  219.1 1.2 bitcast_add_fusion.2
  220.3 1.2 bitcast_add_fusion.2
  221.5 1.2 bitcast_add_fusion.2
  222.7 1.2 bitcast_add_fusion.2
  223.9 1.2 bitcast_add_fusion.2
  225.1 1.2 bitcast_add_fusion.2
  226.3 1.2 bitcast_add_fusion.2
  227.5 1.2 bitcast_add_fusion.2
  229.2 10.6 %all_to_all.18 = bf16[4,128,256]{1,2,0:T(8,128)(2,1)S(1)} all-to-all(bf16[4,128,256]{1,2,0:T(8,128)(2,1)S(1)} %bitcast.22), channel_id=1, replica_groups=mesh['seq'=32,'heads'=4,'dp'=4] {'dp'}, dimensions={0} | all-to-all | bytes 524288 | tf_op jit(solution)/shard_map/all_to_all | solution.py:93
  239.8 0.8 copy.24
  (20 shorter events, 1.8 us)
Async XLA Ops:
  6.5 75.9 %all-gather.4.cloned.1.call-start = ((), (), s32[]{:S(2)}) async-start(), calls=%async_computation.1 | async-start | bytes 4866048 | tf_op jit(solution)/shard_map/all_gather | solution.py:86
  7.3 184.3 %all-gather.6.cloned.1.call-start = ((), (), s32[]{:S(2)}) async-start(), calls=%async_computation.2 | async-start | bytes 17301504 | tf_op jit(solution)/shard_map/all_gather | solution.py:11
  7.3 22.0 %collective-permute-start = (bf16[1,128,3072]{2,1,0:T(8,128)(2,1)}, bf16[1,128,3072]{2,1,0:T(8,128)(2,1)}, u32[]{:S(2)}, u32[]{:S(2)}) collective-permute-start(bf16[1,128,3072]{2,1,0:T(8,128)(2,1)} %param.5), channel_id=1, source_target_pairs={{0,1},{1,2},{2,3},{3,0},{4,5},{5,6},{6,7},{7,4},{8,9},{9,10},{10,1... | collective-permute-start | bytes 2359304 | tf_op jit(solution)/shard_map/ppermute | solution.py:71
  10.5 22.4 %collective-permute-start.1 = (bf16[1,128,3072]{2,1,0:T(8,128)(2,1)}, bf16[1,128,3072]{2,1,0:T(8,128)(2,1)}, u32[]{:S(2)}, u32[]{:S(2)}) collective-permute-start(bf16[1,128,3072]{2,1,0:T(8,128)(2,1)} %param.5), channel_id=1, source_target_pairs={{0,3},{1,0},{2,1},{3,2},{4,7},{5,4},{6,5},{7,6},{8,11},{9,8},{10,9... | collective-permute-start | bytes 2359304 | tf_op jit(solution)/shard_map/ppermute | solution.py:76
  13.9 17.7 %copy-start = (bf16[1,128,3072]{2,1,0:T(8,128)(2,1)S(1)}, bf16[1,128,3072]{2,1,0:T(8,128)(2,1)}, u32[]{:S(2)}) copy-start(bf16[1,128,3072]{2,1,0:T(8,128)(2,1)} %param.5) | copy-start | bytes 2359300
  29.3 21.0 %collective-permute-start.2 = (bf16[1,128,3072]{2,1,0:T(8,128)(2,1)}, bf16[1,128,3072]{2,1,0:T(8,128)(2,1)}, u32[]{:S(2)}, u32[]{:S(2)}) collective-permute-start(bf16[1,128,3072]{2,1,0:T(8,128)(2,1)} %collective-permute-done), channel_id=1, source_target_pairs={{0,1},{1,2},{2,3},{3,0},{4,5},{5,6},{6,7},{7,4},{8,9},{9,10},{10,1... | collective-permute-start | bytes 2359304 | tf_op jit(solution)/shard_map/ppermute | solution.py:71
  191.6 37.4 %copy-start.1 = (f32[256]{0:T(256)S(1)}, f32[256]{0:T(256)}, u32[]{:S(2)}) copy-start(f32[256]{0:T(256)} %param.7) | copy-start | bytes 3076
Sparse Core Ops, SparseCore 0:
  9.5 72.9 all-gather.3
  89.1 102.3 all-gather.5

commit v2 on v0

--- a/solution.py
+++ b/solution.py
@@ -74,7 +74,15 @@
     values_b = to_heads(projected[2].astype(jnp.bfloat16), seq_count, length)
     prefix = block_prefix(keys_b, values_b)
     normed = attend(queries, keys_b, values_b, prefix, norm_gain)
-    return lax.all_to_all(normed, "dp", split_axis=0, concat_axis=2, tiled=True)
+    return jnp.concatenate(
+        lax.all_to_all(
+            jnp.stack(jnp.split(normed, lax.axis_size("dp"), axis=0)),
+            "dp",
+            concat_axis=0,
+            split_axis=0,
+        ),
+        axis=2,
+    )
 
 
 def solution(mesh):

time: 299 us -> 299 us (level)
  no operation moved by 1% of the time
where the time goes in v2:
time: 299 us; the launch traced here: 298 us
  waiting for transfers between devices  227 us (76%)
  other arithmetic  36.5 us (12%)
  between operations  13.2 us (4%)
  blocking collectives  10.6 us (4%)
  matrix products  7.56 us (3%)
    all_gather x1, waiting for transfers between devices, prefix_2(): gathered = lax.all_gather(part, axis)  101 us
    all_gather x1, waiting for transfers between devices, body(): lax.all_gather(proj_weights, 'seq', axis=1, tiled=True)  76.4 us
    all_gather x1, waiting for transfers between devices, body(): everyone = lax.all_gather(tokens, 'dp', axis=0, tiled=True)  47.7 us
    add x31, other arithmetic, add_pair(): return earlier + later  36.3 us
    all_to_all x1, blocking collectives, body(): lax.all_to_all(jnp.stack(jnp.split(normed, lax.axis_size('dp'), axis=0)),...  10.6 us
  transfers between devices with their start and end apart: 3, of which 3 were waited for; matrix products, arithmetic and copies ran while one was open for 0% of the time, Pallas kernels for 0%

profile of v2, /device:TPU:481, one launch (start us, length us, event | category | flops | bytes accessed | tf_op | source)
XLA Modules:
  0.0 297.8 jit_solution(12598075998898996331)
XLA Ops:
  6.5 0.7 all-gather.7.cloned.1.call-update
  7.3 0.7 all-gather.5.cloned.1.call-update
  8.1 47.7 %all-gather.7.cloned.1.call-done = bf16[4,128,3072]{2,1,0:T(8,128)(2,1)} async-done(((bf16[1,128,3072]{2,1,0:T(8,128)(2,1)}), bf16[4,128,3072]{2,1,0:T(8,128)(2,1)}) %all-gather.7.cloned.1.call-update) | async-done | bytes 3145744 | tf_op jit(solution)/shard_map/all_gather | solution.py:63
  55.8 76.4 %all-gather.5.cloned.1.call-done = bf16[3,3072,256]{2,1,0:T(8,128)(2,1)} async-done(((bf16[3,96,256]{2,1,0:T(8,128)(2,1)}), bf16[3,3072,256]{2,1,0:T(8,128)(2,1)}) %all-gather.5.cloned.1.call-update) | async-done | bytes 4718608 | tf_op jit(solution)/shard_map/all_gather | solution.py:70
  132.1 5.5 %convolution_bitcast_fusion = f32[3,512,256]{1,2,0:T(8,128)S(1)} fusion(bf16[3,3072,256]{2,1,0:T(8,128)(2,1)} %all-gather.5.cloned.1.call-done, bf16[512,3072,1]{1,0,2:T(8,128)(2,1)} %bitcast.37), kind=kOutput, calls=%fused_computation.1 | convolution fusion | flops 2415919104 | bytes 9437184 | tf_op jit(solution)/shard_map/nd,jdc->jnc/dot_general | solution.py:27
  137.7 0.2 squeeze.12
  137.9 0.2 copy.16
  138.2 0.2 copy.19
  138.4 1.1 fusion.7
  139.6 0.2 squeeze.11
  139.8 0.2 copy.14
  140.0 0.6 fusion.2
  140.6 101.5 %all-gather.9.cloned.1.call-done = f32[128,2,128,128]{3,2,1,0:T(8,128)} async-done(((f32[4,2,128,128]{3,2,1,0:T(8,128)}), f32[128,2,128,128]{3,2,1,0:T(8,128)}) %all-gather.9.cloned.1.call-update) | async-done | bytes 16777232 | tf_op jit(solution)/shard_map/all_gather | solution.py:11
  242.2 37.0 %while.10 = (s32[]{:T(128)}, f32[4,2,128,128]{3,2,1,0:T(8,128)S(1)}, s32[]{:T(128)}, f32[32,4,2,128,128]{4,3,2,1,0:T(8,128)}, s32[]{:T(128)}, /*index=5*/s32[]{:T(128)}, s32[]{:T(128)}) while((s32[]{:T(128)}, f32[4,2,128,128]{3,2,1,0:T(8,128)S(1)}, s32[]{:T(128)}, f32[32,4,2,128,128]{4,3,2,1,0:T(8,128)}, s32[]{:T(128)}, /*index=5*/s32[]{:T(128)}, ...), condition=%wide.region_1.2_spmd, body=%wide.region_0.1_spmd.sunk | while | flops 131077 | bytes 1572987 | solution.py:17
  242.2 1.2 bitcast_add_fusion.2
  243.4 1.2 bitcast_add_fusion.2
  244.6 1.2 bitcast_add_fusion.2
  245.8 1.2 bitcast_add_fusion.2
  247.0 1.2 bitcast_add_fusion.2
  248.1 1.2 bitcast_add_fusion.2
  249.3 1.2 bitcast_add_fusion.2
  250.5 1.2 bitcast_add_fusion.2
  251.7 1.2 bitcast_add_fusion.2
  252.9 1.2 bitcast_add_fusion.2
  254.1 1.2 bitcast_add_fusion.2
  255.3 1.2 bitcast_add_fusion.2
  256.5 1.2 bitcast_add_fusion.2
  257.7 1.2 bitcast_add_fusion.2
  258.9 1.2 bitcast_add_fusion.2
  260.1 1.2 bitcast_add_fusion.2
  261.3 1.2 bitcast_add_fusion.2
  262.5 1.2 bitcast_add_fusion.2
  263.7 1.2 bitcast_add_fusion.2
  264.9 1.2 bitcast_add_fusion.2
  266.0 1.2 bitcast_add_fusion.2
  267.2 1.2 bitcast_add_fusion.2
  268.4 1.2 bitcast_add_fusion.2
  269.6 1.2 bitcast_add_fusion.2
  270.8 1.2 bitcast_add_fusion.2
  272.0 1.2 bitcast_add_fusion.2
  273.2 1.2 bitcast_add_fusion.2
  274.4 1.2 bitcast_add_fusion.2
  275.6 1.2 bitcast_add_fusion.2
  276.8 1.2 bitcast_add_fusion.2
  278.0 1.2 bitcast_add_fusion.2
  279.2 0.4 multiply_reduce_fusion
  279.7 10.6 %all_to_all.5 = bf16[4,1,128,256]{2,3,1,0:T(8,128)(2,1)S(1)} all-to-all(bf16[4,1,128,256]{2,3,1,0:T(8,128)(2,1)S(1)} %pad_maximum_fusion), channel_id=1, replica_groups=mesh['seq'=32,'heads'=4,'dp'=4] {'dp'}, dimensions={0} | all-to-all | bytes 524288 | tf_op jit(solution)/shard_map/all_to_all | solution.py:78
  290.4 0.8 copy.24
  (15 shorter events, 0.5 us)
Async XLA Ops:
  6.5 49.2 %all-gather.7.cloned.1.call-start = ((), (), s32[]{:S(2)}) async-start(), calls=%async_computation.2 | async-start | bytes 3932160 | tf_op jit(solution)/shard_map/all_gather | solution.py:63
  7.3 124.9 %all-gather.5.cloned.1.call-start = ((), (), s32[]{:S(2)}) async-start(), calls=%async_computation.1 | async-start | bytes 4866048 | tf_op jit(solution)/shard_map/all_gather | solution.py:70
  8.0 234.1 %all-gather.9.cloned.1.call-start = ((), (), s32[]{:S(2)}) async-start(), calls=%async_computation.3 | async-start | bytes 17301504 | tf_op jit(solution)/shard_map/all_gather | solution.py:11
  242.1 37.4 %copy-start = (f32[256]{0:T(256)S(1)}, f32[256]{0:T(256)}, u32[]{:S(2)}) copy-start(f32[256]{0:T(256)} %param.7) | copy-start | bytes 3076
Sparse Core Ops, SparseCore 0:
  9.5 46.2 all-gather.6
  57.9 74.1 all-gather.4
  139.7 102.3 all-gather.8
